TPU v7x, 256 devices: a whole 4x4x8 slice. The times are simulated.
256 devices in a mesh: dp: 2 (over core), expert: 128 (over z, x, y).
Axes of the slice: x: 4, y: 4, z: 8, core: 2. Of those that a mesh axis runs over, the one named last changes fastest.
Arguments:
- out_grad: bfloat16 [16384, 1024], P(('dp', 'expert')), may hold values from -6 to 6
- layer_input: bfloat16 [16384, 1024], P(('dp', 'expert')), may hold values from -6 to 6
- combine: float32 [16384, 8], P(('dp', 'expert')), may hold values from 0.05 to 0.5
- routes: int32 [16384, 8], P(('dp', 'expert')), may hold values from 0 to 127, all different within a row; in each aligned block of 64 rows (0 to 63, 64 to 127, ...) at most 8 rows name the same one
- w_gate_up: bfloat16 [128, 1024, 768], P('expert'), may hold values from -0.1875 to 0.1875
- w_down: bfloat16 [128, 384, 1024], P('expert'), may hold values from -0.3125 to 0.3125
- m_gate_up: float32 [128, 1024, 768], P('expert', 'dp'), may hold values from -0.75 to 0.75
- v_gate_up: float32 [128, 1024, 768], P('expert', 'dp'), may hold values from 0.001 to 0.1
- m_down: float32 [128, 384, 1024], P('expert', None, 'dp'), may hold values from -0.75 to 0.75
- v_down: float32 [128, 384, 1024], P('expert', None, 'dp'), may hold values from 0.001 to 0.1
- swap_pairs: int32 [32, 2], replicated, may hold values from 0 to 127, as said below
Outputs:
- in_grad: bfloat16 [16384, 1024], P(('dp', 'expert'))
- new_gate_up: bfloat16 [128, 1024, 768], P('expert', 'dp')
- new_down: bfloat16 [128, 384, 1024], P('expert', None, 'dp')
- new_m_gate_up: float32 [128, 1024, 768], P('expert', 'dp')
- new_v_gate_up: float32 [128, 1024, 768], P('expert', 'dp')
- new_m_down: float32 [128, 384, 1024], P('expert', None, 'dp')
- new_v_down: float32 [128, 384, 1024], P('expert', None, 'dp')
Inputs may be any that keep to these rules, and one draw needn't show every extreme that they name: `routes`: each row names 8 different experts; among the rows of one device no expert is named more than 8 times, a bound that some block reaches. `swap_pairs`: no device appears twice in the list; devices 0 and 127 are always in it.
All inputs are finite; a program needn't handle non-finite values. Where the computation divides by a largest or mean magnitude, that divisor is 1e-20 or more.
Results may differ from a plain program's by a relative error of at most 0.0064.
Values may be sent and summed in bfloat16 or wider, within the bound.
A program may use at most 128 MiB of HBM per device.

v0:
```python
import jax
import jax.numpy as jnp
from jax import lax
from jax.sharding import PartitionSpec as P

BETA_ONE = 0.9
BETA_TWO = 0.95
RATE = 0.001
DECAY = 0.1
ADAM_EPS = 1e-08
PEAK_EPS = 1e-06


def partner_table(swap_pairs, expert_count):
    devices = jnp.arange(expert_count, dtype=jnp.int32)
    first_dev = swap_pairs[:, 0]
    second_dev = swap_pairs[:, 1]
    hit_first = devices[:, None] == first_dev[None, :]
    hit_second = devices[:, None] == second_dev[None, :]
    other = jnp.sum(
        jnp.where(hit_first, second_dev[None, :], 0) + jnp.where(hit_second, first_dev[None, :], 0),
        axis=1,
    )
    paired = jnp.any(hit_first | hit_second, axis=1)
    return jnp.where(paired, other, devices)


def slot_ranks(route_ids, expert_count):
    flat_ids = route_ids.reshape(-1)
    onehot = (flat_ids[:, None] == jnp.arange(expert_count, dtype=jnp.int32)[None, :]).astype(
        jnp.int32
    )
    before = jnp.cumsum(onehot, axis=0) - onehot
    return jnp.sum(before * onehot, axis=1)


def expert_backward(slot_grad, slot_input, gate_up, down_proj):
    hidden_units = down_proj.shape[0]
    pre_act = jnp.dot(slot_input, gate_up, preferred_element_type=jnp.float32)
    gate_pre = pre_act[:, :hidden_units]
    up_pre = pre_act[:, hidden_units:]
    sigmoid_gate = jax.nn.sigmoid(gate_pre)
    gate_act = gate_pre * sigmoid_gate
    hidden = (gate_act * up_pre).astype(jnp.bfloat16)
    d_hidden = lax.dot_general(
        slot_grad, down_proj, (((1,), (1,)), ((), ())), preferred_element_type=jnp.float32
    )
    d_gate = d_hidden * up_pre * sigmoid_gate * (1.0 + gate_pre * (1.0 - sigmoid_gate))
    d_up = d_hidden * gate_act
    d_pre = jnp.concatenate([d_gate, d_up], axis=1).astype(jnp.bfloat16)
    grad_down = lax.dot_general(
        hidden, slot_grad, (((0,), (0,)), ((), ())), preferred_element_type=jnp.float32
    )
    grad_gate_up = lax.dot_general(
        slot_input, d_pre, (((0,), (0,)), ((), ())), preferred_element_type=jnp.float32
    )
    slot_back = lax.dot_general(
        d_pre, gate_up, (((1,), (1,)), ((), ())), preferred_element_type=jnp.float32
    ).astype(jnp.bfloat16)
    return (slot_back, grad_gate_up, grad_down)


def adam_update(weight, grad, mean_in, square_in, scale_by):
    scaled = grad * scale_by
    mean_new = BETA_ONE * mean_in + (1.0 - BETA_ONE) * scaled
    square_new = BETA_TWO * square_in + (1.0 - BETA_TWO) * scaled * scaled
    weight_wide = weight.astype(jnp.float32)
    step_size = mean_new / (jnp.sqrt(square_new) + ADAM_EPS)
    weight_new = (weight_wide - RATE * (step_size + DECAY * weight_wide)).astype(jnp.bfloat16)
    return (weight_new, mean_new, square_new)


def move_moments(gate_mean, gate_square, down_mean, down_square, partner):
    expert_count = partner.shape[0]
    spread_out = (
        lax.all_to_all(
            gate_mean.reshape(1, expert_count, -1),
            "expert",
            split_axis=1,
            concat_axis=0,
            tiled=True,
        ),
        lax.all_to_all(
            gate_square.reshape(1, expert_count, -1),
            "expert",
            split_axis=1,
            concat_axis=0,
            tiled=True,
        ),
        lax.all_to_all(
            down_mean.reshape(1, expert_count, -1),
            "expert",
            split_axis=1,
            concat_axis=0,
            tiled=True,
        ),
        lax.all_to_all(
            down_square.reshape(1, expert_count, -1),
            "expert",
            split_axis=1,
            concat_axis=0,
            tiled=True,
        ),
    )
    picked = [jnp.take(element, partner, axis=0) for element in spread_out]
    arrived = (
        lax.all_to_all(picked[0], "expert", split_axis=0, concat_axis=1, tiled=True),
        lax.all_to_all(picked[1], "expert", split_axis=0, concat_axis=1, tiled=True),
        lax.all_to_all(picked[2], "expert", split_axis=0, concat_axis=1, tiled=True),
        lax.all_to_all(picked[3], "expert", split_axis=0, concat_axis=1, tiled=True),
    )
    return (
        arrived[0].reshape(gate_mean.shape),
        arrived[1].reshape(gate_square.shape),
        arrived[2].reshape(down_mean.shape),
        arrived[3].reshape(down_square.shape),
    )


def move_weights_after(gate_up, down_proj, partner):
    expert_count = partner.shape[0]
    spread_out = (
        lax.all_to_all(
            gate_up.reshape(1, expert_count, -1), "expert", split_axis=1, concat_axis=0, tiled=True
        ),
        lax.all_to_all(
            down_proj.reshape(1, expert_count, -1),
            "expert",
            split_axis=1,
            concat_axis=0,
            tiled=True,
        ),
    )
    picked = [jnp.take(element, partner, axis=0) for element in spread_out]
    arrived = (
        lax.all_to_all(picked[0], "expert", split_axis=0, concat_axis=1, tiled=True),
        lax.all_to_all(picked[1], "expert", split_axis=0, concat_axis=1, tiled=True),
    )
    return (arrived[0].reshape(gate_up.shape), arrived[1].reshape(down_proj.shape))


def per_device(
    out_grad,
    layer_input,
    combine,
    routes,
    w_gate_up,
    w_down,
    m_gate_up,
    v_gate_up,
    m_down,
    v_down,
    swap_pairs,
):
    expert_count = lax.axis_size("expert")
    replicas = lax.axis_size("dp")
    replica = lax.axis_index("dp")
    partner = partner_table(swap_pairs, expert_count)
    tok_rows, top_count = routes.shape
    capacity = 2 * tok_rows * top_count // expert_count
    model_width = out_grad.shape[1]
    ranks = slot_ranks(routes, expert_count)
    assign = tok_rows * top_count
    slot_place = routes.reshape(-1) * capacity + ranks
    slot_owner = (
        jnp.full((expert_count * capacity,), -1, jnp.int32)
        .at[slot_place]
        .set(jnp.arange(assign, dtype=jnp.int32))
    )
    is_live = slot_owner >= 0
    safe_index = jnp.maximum(slot_owner, 0)
    token_ids = safe_index // top_count
    weights = jnp.where(is_live, combine.reshape(-1)[safe_index], jnp.float32(0.0))
    slot_grad = (out_grad[token_ids].astype(jnp.float32) * weights[:, None]).astype(jnp.bfloat16)
    slot_input = jnp.where(is_live[:, None], layer_input[token_ids], jnp.zeros((), jnp.bfloat16))
    slot_grad, slot_input = (
        lax.all_to_all(
            slot_grad.reshape(expert_count, capacity, model_width),
            "expert",
            split_axis=0,
            concat_axis=0,
            tiled=True,
        ),
        lax.all_to_all(
            slot_input.reshape(expert_count, capacity, model_width),
            "expert",
            split_axis=0,
            concat_axis=0,
            tiled=True,
        ),
    )
    slot_back, grad_gate_up, grad_down = expert_backward(
        slot_grad.reshape(-1, model_width),
        slot_input.reshape(-1, model_width),
        w_gate_up[0],
        w_down[0],
    )
    slot_back = lax.all_to_all(
        slot_back.reshape(expert_count, capacity, model_width),
        "expert",
        split_axis=0,
        concat_axis=0,
        tiled=True,
    )
    returned = slot_back.reshape(expert_count * capacity, model_width)[slot_place].reshape(
        tok_rows, top_count, model_width
    )
    in_grad = jnp.sum(returned, axis=1, dtype=jnp.float32).astype(jnp.bfloat16)
    half_rows = model_width // replicas
    part_gate_up, part_down = (
        lax.psum_scatter(
            grad_gate_up.astype(jnp.bfloat16), "dp", scatter_dimension=0, tiled=True
        ).astype(jnp.float32),
        lax.psum_scatter(
            grad_down.astype(jnp.bfloat16), "dp", scatter_dimension=1, tiled=True
        ).astype(jnp.float32),
    )
    local_peak = jnp.maximum(jnp.max(jnp.abs(part_gate_up)), jnp.max(jnp.abs(part_down)))
    peak_abs = lax.pmax(local_peak, "dp")
    scale_by = 1.0 / (peak_abs + PEAK_EPS)
    own_gate_up = lax.dynamic_slice_in_dim(w_gate_up[0], replica * half_rows, half_rows, 0)
    own_down = lax.dynamic_slice_in_dim(w_down[0], replica * half_rows, half_rows, 1)
    new_gu, gate_mean, gate_square = adam_update(
        own_gate_up, part_gate_up, m_gate_up[0], v_gate_up[0], scale_by
    )
    new_dn, down_mean, down_square = adam_update(
        own_down, part_down, m_down[0], v_down[0], scale_by
    )
    new_gu, new_dn = move_weights_after(new_gu, new_dn, partner)
    gate_mean, gate_square, down_mean, down_square = move_moments(
        gate_mean, gate_square, down_mean, down_square, partner
    )
    return (
        in_grad,
        new_gu[None],
        new_dn[None],
        gate_mean[None],
        gate_square[None],
        down_mean[None],
        down_square[None],
    )


def solution(mesh):
    in_specs = (
        P(("dp", "expert"), None),
        P(("dp", "expert"), None),
        P(("dp", "expert"), None),
        P(("dp", "expert"), None),
        P("expert", None, None),
        P("expert", None, None),
        P("expert", "dp", None),
        P("expert", "dp", None),
        P("expert", None, "dp"),
        P("expert", None, "dp"),
        P(),
    )
    out_specs = (
        P(("dp", "expert"), None),
        P("expert", "dp", None),
        P("expert", None, "dp"),
        P("expert", "dp", None),
        P("expert", "dp", None),
        P("expert", None, "dp"),
        P("expert", None, "dp"),
    )
    return jax.shard_map(
        per_device, mesh=mesh, in_specs=in_specs, out_specs=out_specs, check_vma=False
    )
```

profile of v0, /device:TPU:2, one launch (start us, length us, event | category | flops | bytes accessed | tf_op | source)
XLA Modules:
  0.0 669.4 jit_solution(3657734862248697985)
XLA Ops:
  25.7 16.0 %all-to-all-start.1 = ((bf16[128,8,1024]{2,1,0:T(8,128)(2,1)}), bf16[128,8,1024]{2,1,0:T(8,128)(2,1)}, u32[]{:S(2)}, u32[]{:S(2)}) async-start(bf16[128,8,1024]{2,1,0:T(8,128)(2,1)} %bitcast_select_fusion), calls=%async_computation.1 | async-start | bytes 4194304 | tf_op jit(solution)/shard_map/all_to_all | solution.py:184
  47.7 46.3 %all-to-all-done.1 = bf16[128,8,1024]{2,1,0:T(8,128)(2,1)} async-done(((bf16[128,8,1024]{2,1,0:T(8,128)(2,1)}), bf16[128,8,1024]{2,1,0:T(8,128)(2,1)}, u32[]{:S(2)}, u32[]{:S(2)}) %all-to-all-start.1) | async-done | bytes 2097184 | tf_op jit(solution)/shard_map/all_to_all | solution.py:184
  106.9 46.3 %all-to-all-done = bf16[128,8,1024]{2,1,0:T(8,128)(2,1)S(1)} async-done(((bf16[128,8,1024]{2,1,0:T(8,128)(2,1)}), bf16[128,8,1024]{2,1,0:T(8,128)(2,1)S(1)}, u32[]{:S(2)}, u32[]{:S(2)}) %all-to-all-start) | async-done | bytes 2097184 | tf_op jit(solution)/shard_map/all_to_all | solution.py:177
  168.1 16.2 %reduce-scatter.3.cloned.1.call-done = bf16[512,768]{1,0:T(8,128)(2,1)} async-done(((bf16[1024,768]{1,0:T(8,128)(2,1)}), bf16[512,768]{1,0:T(8,128)(2,1)}) %reduce-scatter.3.cloned.1.call-update) | async-done | bytes 786448 | tf_op jit(solution)/shard_map/reduce_scatter | solution.py:211
  198.4 13.8 %all-to-all-start.5 = ((bf16[128,2,768]{2,1,0:T(2,128)(2,1)}), bf16[128,2,768]{2,1,0:T(2,128)(2,1)S(1)}, u32[]{:S(2)}, u32[]{:S(2)}) async-start(bf16[128,2,768]{2,1,0:T(2,128)(2,1)} %reshape.474), calls=%async_computation.7 | async-start | bytes 786432 | tf_op jit(solution)/shard_map/all_to_all | solution.py:126
  217.0 12.9 %all-to-all-done.5 = bf16[128,2,768]{2,1,0:T(2,128)(2,1)S(1)} async-done(((bf16[128,2,768]{2,1,0:T(2,128)(2,1)}), bf16[128,2,768]{2,1,0:T(2,128)(2,1)S(1)}, u32[]{:S(2)}, u32[]{:S(2)}) %all-to-all-start.5) | async-done | bytes 393248 | tf_op jit(solution)/shard_map/all_to_all | solution.py:126
  240.8 48.4 %all-to-all-done.2 = bf16[128,8,1024]{2,1,0:T(8,128)(2,1)S(1)} async-done(((bf16[128,8,1024]{2,1,0:T(8,128)(2,1)}), bf16[128,8,1024]{2,1,0:T(8,128)(2,1)S(1)}, u32[]{:S(2)}, u32[]{:S(2)}) %all-to-all-start.2) | async-done | bytes 2097184 | tf_op jit(solution)/shard_map/all_to_all | solution.py:198
  289.1 7.5 %all-to-all-start.13 = ((f32[1,128,1536]{2,0,1:T(1,128)}), f32[1,128,1536]{2,0,1:T(1,128)}, u32[]{:S(2)}, u32[]{:S(2)}) async-start(f32[1,128,1536]{2,0,1:T(1,128)} %reshape.460), calls=%async_computation.15 | async-start | bytes 1572864 | tf_op jit(solution)/shard_map/all_to_all | solution.py:97
  298.5 21.6 %all-to-all-done.13 = f32[1,128,1536]{2,0,1:T(1,128)} async-done(((f32[1,128,1536]{2,0,1:T(1,128)}), f32[1,128,1536]{2,0,1:T(1,128)}, u32[]{:S(2)}, u32[]{:S(2)}) %all-to-all-start.13) | async-done | bytes 786464 | tf_op jit(solution)/shard_map/all_to_all | solution.py:97
  320.0 8.0 %all-to-all-start.11 = ((f32[1,128,1536]{2,0,1:T(1,128)}), f32[1,128,1536]{2,0,1:T(1,128)}, u32[]{:S(2)}, u32[]{:S(2)}) async-start(f32[1,128,1536]{2,0,1:T(1,128)} %reshape.458), calls=%async_computation.13 | async-start | bytes 1572864 | tf_op jit(solution)/shard_map/all_to_all | solution.py:90
  350.2 10.9 %all-to-all-start.3 = ((bf16[128,2,1536]{2,1,0:T(2,128)(2,1)}), bf16[128,2,1536]{2,1,0:T(2,128)(2,1)}, u32[]{:S(2)}, u32[]{:S(2)}) async-start(bf16[128,2,1536]{2,1,0:T(2,128)(2,1)} %reshape.470), calls=%async_computation.5 | async-start | bytes 1572864 | tf_op jit(solution)/shard_map/all_to_all | solution.py:123
  364.6 18.3 %all-to-all-done.3 = bf16[128,2,1536]{2,1,0:T(2,128)(2,1)} async-done(((bf16[128,2,1536]{2,1,0:T(2,128)(2,1)}), bf16[128,2,1536]{2,1,0:T(2,128)(2,1)}, u32[]{:S(2)}, u32[]{:S(2)}) %all-to-all-start.3) | async-done | bytes 786464 | tf_op jit(solution)/shard_map/all_to_all | solution.py:123
  382.8 7.9 %all-to-all-start.6 = ((bf16[128,2,768]{2,1,0:T(2,128)(2,1)}), bf16[128,2,768]{2,1,0:T(2,128)(2,1)}, u32[]{:S(2)}, u32[]{:S(2)}) async-start(bf16[128,2,768]{2,1,0:T(2,128)(2,1)} %reshape.476), calls=%async_computation.8 | async-start | bytes 786432 | tf_op jit(solution)/shard_map/all_to_all | solution.py:137
  405.1 8.8 %all-to-all-start.14 = ((f32[128,1,1536]{2,1,0:T(1,128)}), f32[128,1,1536]{2,1,0:T(1,128)}, u32[]{:S(2)}, u32[]{:S(2)}) async-start(f32[128,1,1536]{2,1,0:T(1,128)} %copy.77), calls=%async_computation.16 | async-start | bytes 1572864 | tf_op jit(solution)/shard_map/all_to_all | solution.py:110
  416.9 16.9 %all-to-all-done.14 = f32[128,1,1536]{2,1,0:T(1,128)} async-done(((f32[128,1,1536]{2,1,0:T(1,128)}), f32[128,1,1536]{2,1,0:T(1,128)}, u32[]{:S(2)}, u32[]{:S(2)}) %all-to-all-start.14) | async-done | bytes 786464 | tf_op jit(solution)/shard_map/all_to_all | solution.py:110
  433.8 7.7 %all-to-all-start.12 = ((f32[128,1,1536]{2,1,0:T(1,128)}), f32[128,1,1536]{2,1,0:T(1,128)}, u32[]{:S(2)}, u32[]{:S(2)}) async-start(f32[128,1,1536]{2,1,0:T(1,128)} %copy.75), calls=%async_computation.14 | async-start | bytes 1572864 | tf_op jit(solution)/shard_map/all_to_all | solution.py:109
  444.2 16.0 %all-to-all-done.12 = f32[128,1,1536]{2,1,0:T(1,128)} async-done(((f32[128,1,1536]{2,1,0:T(1,128)}), f32[128,1,1536]{2,1,0:T(1,128)}, u32[]{:S(2)}, u32[]{:S(2)}) %all-to-all-start.12) | async-done | bytes 786464 | tf_op jit(solution)/shard_map/all_to_all | solution.py:109
  470.2 31.2 %all-to-all-done.9 = f32[1,128,3072]{2,0,1:T(1,128)S(1)} async-done(((f32[1,128,3072]{2,0,1:T(1,128)}), f32[1,128,3072]{2,0,1:T(1,128)S(1)}, u32[]{:S(2)}, u32[]{:S(2)}) %all-to-all-start.9) | async-done | bytes 1572896 | tf_op jit(solution)/shard_map/all_to_all | solution.py:83
  520.3 23.0 %all-to-all-done.7 = f32[1,128,3072]{2,0,1:T(1,128)} async-done(((f32[1,128,3072]{2,0,1:T(1,128)}), f32[1,128,3072]{2,0,1:T(1,128)}, u32[]{:S(2)}, u32[]{:S(2)}) %all-to-all-start.7) | async-done | bytes 1572896 | tf_op jit(solution)/shard_map/all_to_all | solution.py:76
  543.4 7.5 %all-to-all-start.4 = ((bf16[128,2,1536]{2,1,0:T(2,128)(2,1)}), bf16[128,2,1536]{2,1,0:T(2,128)(2,1)}, u32[]{:S(2)}, u32[]{:S(2)}) async-start(bf16[128,2,1536]{2,1,0:T(2,128)(2,1)} %reshape.472), calls=%async_computation.6 | async-start | bytes 1572864 | tf_op jit(solution)/shard_map/all_to_all | solution.py:136
  560.9 9.3 %all-to-all-done.4 = bf16[128,2,1536]{2,1,0:T(2,128)(2,1)} async-done(((bf16[128,2,1536]{2,1,0:T(2,128)(2,1)}), bf16[128,2,1536]{2,1,0:T(2,128)(2,1)}, u32[]{:S(2)}, u32[]{:S(2)}) %all-to-all-start.4) | async-done | bytes 786464 | tf_op jit(solution)/shard_map/all_to_all | solution.py:136
  570.2 7.9 %all-to-all-start.10 = ((f32[128,1,3072]{2,1,0:T(1,128)}), f32[128,1,3072]{2,1,0:T(1,128)}, u32[]{:S(2)}, u32[]{:S(2)}) async-start(f32[128,1,3072]{2,1,0:T(1,128)} %copy.73), calls=%async_computation.12 | async-start | bytes 3145728 | tf_op jit(solution)/shard_map/all_to_all | solution.py:108
  580.8 31.5 %all-to-all-done.10 = f32[128,1,3072]{2,1,0:T(1,128)} async-done(((f32[128,1,3072]{2,1,0:T(1,128)}), f32[128,1,3072]{2,1,0:T(1,128)}, u32[]{:S(2)}, u32[]{:S(2)}) %all-to-all-start.10) | async-done | bytes 1572896 | tf_op jit(solution)/shard_map/all_to_all | solution.py:108
  612.3 7.5 %all-to-all-start.8 = ((f32[128,1,3072]{2,1,0:T(1,128)}), f32[128,1,3072]{2,1,0:T(1,128)}, u32[]{:S(2)}, u32[]{:S(2)}) async-start(f32[128,1,3072]{2,1,0:T(1,128)} %copy.71), calls=%async_computation.10 | async-start | bytes 3145728 | tf_op jit(solution)/shard_map/all_to_all | solution.py:107
  (144 shorter events, 211.0 us)
Async XLA Ops:
  25.7 68.3 %all-to-all-start.1 = ((bf16[128,8,1024]{2,1,0:T(8,128)(2,1)}), bf16[128,8,1024]{2,1,0:T(8,128)(2,1)}, u32[]{:S(2)}, u32[]{:S(2)}) async-start(bf16[128,8,1024]{2,1,0:T(8,128)(2,1)} %bitcast_select_fusion), calls=%async_computation.1 | async-start | bytes 4194304 | tf_op jit(solution)/shard_map/all_to_all | solution.py:184
  94.0 59.1 %all-to-all-start = ((bf16[128,8,1024]{2,1,0:T(8,128)(2,1)}), bf16[128,8,1024]{2,1,0:T(8,128)(2,1)S(1)}, u32[]{:S(2)}, u32[]{:S(2)}) async-start(bf16[128,8,1024]{2,1,0:T(8,128)(2,1)} %fusion), calls=%async_computation | async-start | bytes 4194304 | tf_op jit(solution)/shard_map/all_to_all | solution.py:177
  101.3 65.1 %reduce-scatter.5.cloned.1.call-start = ((), (), s32[]{:S(2)}) async-start(), calls=%async_computation.18 | async-start | bytes 1179648 | tf_op jit(solution)/shard_map/reduce_scatter | solution.py:214
  106.9 50.3 %copy-start.11 = (bf16[1,384,1024]{2,1,0:T(8,128)(2,1)S(1)}, bf16[1,384,1024]{2,1,0:T(8,128)(2,1)}, u32[]{:S(2)}) copy-start(bf16[1,384,1024]{2,1,0:T(8,128)(2,1)} %param.20) | copy-start | bytes 2359300
  156.9 27.4 %reduce-scatter.3.cloned.1.call-start = ((), (), s32[]{:S(2)}) async-start(), calls=%async_computation.17 | async-start | bytes 2359296 | tf_op jit(solution)/shard_map/reduce_scatter | solution.py:211
  166.3 24.9 %copy-start.9 = (f32[1,384,512]{2,1,0:T(8,128)S(1)}, f32[1,384,512]{2,1,0:T(8,128)}, u32[]{:S(2)}) copy-start(f32[1,384,512]{2,1,0:T(8,128)} %param.24) | copy-start | bytes 2359300
  166.3 24.9 %copy-start.10 = (f32[1,384,512]{2,1,0:T(8,128)S(1)}, f32[1,384,512]{2,1,0:T(8,128)}, u32[]{:S(2)}) copy-start(f32[1,384,512]{2,1,0:T(8,128)} %param.23) | copy-start | bytes 2359300
  194.0 18.1 %copy-start.14 = (bf16[1024,384]{0,1:T(8,128)(2,1)S(1)}, bf16[1024,384]{0,1:T(8,128)(2,1)}, u32[]{:S(2)}) copy-start(bf16[1024,384]{0,1:T(8,128)(2,1)} %copy-done.13) | copy-start | bytes 2359300
  198.4 31.6 %all-to-all-start.5 = ((bf16[128,2,768]{2,1,0:T(2,128)(2,1)}), bf16[128,2,768]{2,1,0:T(2,128)(2,1)S(1)}, u32[]{:S(2)}, u32[]{:S(2)}) async-start(bf16[128,2,768]{2,1,0:T(2,128)(2,1)} %reshape.474), calls=%async_computation.7 | async-start | bytes 786432 | tf_op jit(solution)/shard_map/all_to_all | solution.py:126
  230.7 58.4 %all-to-all-start.2 = ((bf16[128,8,1024]{2,1,0:T(8,128)(2,1)}), bf16[128,8,1024]{2,1,0:T(8,128)(2,1)S(1)}, u32[]{:S(2)}, u32[]{:S(2)}) async-start(bf16[128,8,1024]{2,1,0:T(8,128)(2,1)} %convert_bitcast_fusion), calls=%async_computation.2 | async-start | bytes 4194304 | tf_op jit(solution)/shard_map/all_to_all | solution.py:198
  289.1 30.9 %all-to-all-start.13 = ((f32[1,128,1536]{2,0,1:T(1,128)}), f32[1,128,1536]{2,0,1:T(1,128)}, u32[]{:S(2)}, u32[]{:S(2)}) async-start(f32[1,128,1536]{2,0,1:T(1,128)} %reshape.460), calls=%async_computation.15 | async-start | bytes 1572864 | tf_op jit(solution)/shard_map/all_to_all | solution.py:97
  298.5 29.6 %copy-start.6 = (bf16[512,768]{1,0:T(8,128)(2,1)S(1)}, bf16[512,768]{1,0:T(8,128)(2,1)}, u32[]{:S(2)}) copy-start(bf16[512,768]{1,0:T(8,128)(2,1)} %reduce-scatter.3.cloned.1.call-done) | copy-start | bytes 2359300
  320.0 30.2 %all-to-all-start.11 = ((f32[1,128,1536]{2,0,1:T(1,128)}), f32[1,128,1536]{2,0,1:T(1,128)}, u32[]{:S(2)}, u32[]{:S(2)}) async-start(f32[1,128,1536]{2,0,1:T(1,128)} %reshape.458), calls=%async_computation.13 | async-start | bytes 1572864 | tf_op jit(solution)/shard_map/all_to_all | solution.py:90
  350.2 32.6 %all-to-all-start.3 = ((bf16[128,2,1536]{2,1,0:T(2,128)(2,1)}), bf16[128,2,1536]{2,1,0:T(2,128)(2,1)}, u32[]{:S(2)}, u32[]{:S(2)}) async-start(bf16[128,2,1536]{2,1,0:T(2,128)(2,1)} %reshape.470), calls=%async_computation.5 | async-start | bytes 1572864 | tf_op jit(solution)/shard_map/all_to_all | solution.py:123
  382.8 22.2 %all-to-all-start.6 = ((bf16[128,2,768]{2,1,0:T(2,128)(2,1)}), bf16[128,2,768]{2,1,0:T(2,128)(2,1)}, u32[]{:S(2)}, u32[]{:S(2)}) async-start(bf16[128,2,768]{2,1,0:T(2,128)(2,1)} %reshape.476), calls=%async_computation.8 | async-start | bytes 786432 | tf_op jit(solution)/shard_map/all_to_all | solution.py:137
  405.1 28.7 %all-to-all-start.14 = ((f32[128,1,1536]{2,1,0:T(1,128)}), f32[128,1,1536]{2,1,0:T(1,128)}, u32[]{:S(2)}, u32[]{:S(2)}) async-start(f32[128,1,1536]{2,1,0:T(1,128)} %copy.77), calls=%async_computation.16 | async-start | bytes 1572864 | tf_op jit(solution)/shard_map/all_to_all | solution.py:110
  413.9 27.6 %copy-start.5 = (f32[512,768]{1,0:T(8,128)S(1)}, f32[512,768]{1,0:T(8,128)}, u32[]{:S(2)}) copy-start(f32[512,768]{1,0:T(8,128)} %get-tuple-element.15) | copy-start | bytes 4718596
  433.8 26.4 %all-to-all-start.12 = ((f32[128,1,1536]{2,1,0:T(1,128)}), f32[128,1,1536]{2,1,0:T(1,128)}, u32[]{:S(2)}, u32[]{:S(2)}) async-start(f32[128,1,1536]{2,1,0:T(1,128)} %copy.75), calls=%async_computation.14 | async-start | bytes 1572864 | tf_op jit(solution)/shard_map/all_to_all | solution.py:109
  460.2 41.2 %all-to-all-start.9 = ((f32[1,128,3072]{2,0,1:T(1,128)}), f32[1,128,3072]{2,0,1:T(1,128)S(1)}, u32[]{:S(2)}, u32[]{:S(2)}) async-start(f32[1,128,3072]{2,0,1:T(1,128)} %reshape.456), calls=%async_computation.11 | async-start | bytes 3145728 | tf_op jit(solution)/shard_map/all_to_all | solution.py:83
  501.4 42.0 %all-to-all-start.7 = ((f32[1,128,3072]{2,0,1:T(1,128)}), f32[1,128,3072]{2,0,1:T(1,128)}, u32[]{:S(2)}, u32[]{:S(2)}) async-start(f32[1,128,3072]{2,0,1:T(1,128)} %reshape.454), calls=%async_computation.9 | async-start | bytes 3145728 | tf_op jit(solution)/shard_map/all_to_all | solution.py:76
  543.4 26.8 %all-to-all-start.4 = ((bf16[128,2,1536]{2,1,0:T(2,128)(2,1)}), bf16[128,2,1536]{2,1,0:T(2,128)(2,1)}, u32[]{:S(2)}, u32[]{:S(2)}) async-start(bf16[128,2,1536]{2,1,0:T(2,128)(2,1)} %reshape.472), calls=%async_computation.6 | async-start | bytes 1572864 | tf_op jit(solution)/shard_map/all_to_all | solution.py:136
  570.2 42.1 %all-to-all-start.10 = ((f32[128,1,3072]{2,1,0:T(1,128)}), f32[128,1,3072]{2,1,0:T(1,128)}, u32[]{:S(2)}, u32[]{:S(2)}) async-start(f32[128,1,3072]{2,1,0:T(1,128)} %copy.73), calls=%async_computation.12 | async-start | bytes 3145728 | tf_op jit(solution)/shard_map/all_to_all | solution.py:108
  580.8 39.0 %copy-start.4 = (bf16[128,8,1024]{2,1,0:T(8,128)(2,1)S(1)}, bf16[128,8,1024]{2,1,0:T(8,128)(2,1)}, u32[]{:S(2)}) copy-start(bf16[128,8,1024]{2,1,0:T(8,128)(2,1)} %copy-done.3) | copy-start | bytes 6291460
  612.3 43.1 %all-to-all-start.8 = ((f32[128,1,3072]{2,1,0:T(1,128)}), f32[128,1,3072]{2,1,0:T(1,128)}, u32[]{:S(2)}, u32[]{:S(2)}) async-start(f32[128,1,3072]{2,1,0:T(1,128)} %copy.71), calls=%async_computation.10 | async-start | bytes 3145728 | tf_op jit(solution)/shard_map/all_to_all | solution.py:107
  (9 other events, 83.2 us)
Sparse Core Ops, SparseCore 0:
  157.1 8.2 reduce-scatter.4
  168.6 15.7 reduce-scatter.2
where the time goes:
time: 679 us; the launch traced here: 669 us
  waiting for transfers between devices  347 us (51%)
  starting transfers between devices  133 us (20%)
  local copies, waits for them, and re-layouts  91.6 us (13%)
  other arithmetic  56.2 us (8%)
  matrix products  22.1 us (3%)
  between operations  17 us (3%)
    all_to_all x1, waiting for transfers between devices, per_device(): lax.all_to_all(slot_back.reshape(expert_count, capacity, model_width), 'e...  48.4 us
    all_to_all x1, waiting for transfers between devices, per_device(): lax.all_to_all(slot_input.reshape(expert_count, capacity, model_width), '...  46.3 us
    all_to_all x1, waiting for transfers between devices, per_device(): lax.all_to_all(slot_grad.reshape(expert_count, capacity, model_width), 'e...  46.3 us
    all_to_all x1, waiting for transfers between devices, move_moments(): lax.all_to_all(picked[1], 'expert', split_axis=0, concat_axis=1, tiled=True)  31.5 us
    all_to_all x1, waiting for transfers between devices, move_moments(): lax.all_to_all(gate_square.reshape(1, expert_count, -1), 'expert', split_...  31.2 us
    unnamed x50, local copies, waits for them, and re-layouts  30.7 us
    all_to_all x1, waiting for transfers between devices, move_moments(): lax.all_to_all(gate_mean.reshape(1, expert_count, -1), 'expert', split_ax...  23 us
    all_to_all x1, waiting for transfers between devices, move_moments(): lax.all_to_all(down_square.reshape(1, expert_count, -1), 'expert', split_...  21.6 us
  transfers between devices with their start and end apart: 17, of which 15 were waited for; matrix products, arithmetic and copies ran while one was open for 19% of the time, Pallas kernels for 0%

commit v1 on v0

--- a/solution.py
+++ b/solution.py
@@ -73,12 +73,18 @@
 def move_moments(gate_mean, gate_square, down_mean, down_square, partner):
     expert_count = partner.shape[0]
     spread_out = (
-        lax.all_to_all(
-            gate_mean.reshape(1, expert_count, -1),
-            "expert",
-            split_axis=1,
-            concat_axis=0,
-            tiled=True,
+        jnp.concatenate(
+            lax.all_to_all(
+                jnp.stack(
+                    jnp.split(
+                        gate_mean.reshape(1, expert_count, -1), lax.axis_size("expert"), axis=1
+                    )
+                ),
+                "expert",
+                0,
+                0,
+            ),
+            axis=0,
         ),
         lax.all_to_all(
             gate_square.reshape(1, expert_count, -1),

time: 679 us -> 757 us (1.11)
  local copies, waits for them, and re-layouts: 91.6 us -> 178 us
    unnamed x50 -> x193, local copies, waits for them, and re-layouts: 30.7 us -> 124 us
    all_to_all x1, waiting for transfers between devices: 12.9 us -> 0.01 us  [move_weights_after(): lax.all_to_all(down_proj.reshape(1, expert_count, -1), 'expert', split_ax...]
    all_to_all x1, waiting for transfers between devices: 23 us -> 34.4 us  [move_moments(): lax.all_to_all(jnp.stack(jnp.split(gate_mean.reshape(1, expert_count, -1)...]
    all_to_all x1, waiting for transfers between devices: 48.4 us -> 39.1 us  [per_device(): lax.all_to_all(slot_back.reshape(expert_count, capacity, model_width), 'e...]
    all_to_all x1, waiting for transfers between devices: 3.34 us -> 11.4 us  [move_moments(): lax.all_to_all(down_mean.reshape(1, expert_count, -1), 'expert', split_ax...]
  transfers between devices with their start and end apart: 17 -> 17, of which waited for: 15 -> 15; matrix products, arithmetic and copies ran while one was open for 19% -> 28% of each run, Pallas kernels for 0% -> 0%
where the time goes in v1:
time: 757 us; the launch traced here: 746 us
  waiting for transfers between devices  342 us (45%)
  local copies, waits for them, and re-layouts  178 us (24%)
  starting transfers between devices  133 us (18%)
  other arithmetic  50.8 us (7%)
  matrix products  22.4 us (3%)
  between operations  17.1 us (2%)
    unnamed x193, local copies, waits for them, and re-layouts  124 us
    all_to_all x1, waiting for transfers between devices, per_device(): lax.all_to_all(slot_grad.reshape(expert_count, capacity, model_width), 'e...  46.3 us
    all_to_all x1, waiting for transfers between devices, per_device(): lax.all_to_all(slot_input.reshape(expert_count, capacity, model_width), '...  46.3 us
    all_to_all x1, waiting for transfers between devices, per_device(): lax.all_to_all(slot_back.reshape(expert_count, capacity, model_width), 'e...  39.1 us
    all_to_all x1, waiting for transfers between devices, move_moments(): lax.all_to_all(jnp.stack(jnp.split(gate_mean.reshape(1, expert_count, -1)...  34.4 us
    all_to_all x1, waiting for transfers between devices, move_moments(): lax.all_to_all(picked[1], 'expert', split_axis=0, concat_axis=1, tiled=True)  33.3 us
    all_to_all x1, waiting for transfers between devices, move_moments(): lax.all_to_all(gate_square.reshape(1, expert_count, -1), 'expert', split_...  29.2 us
    all_to_all x1, waiting for transfers between devices, move_moments(): lax.all_to_all(down_square.reshape(1, expert_count, -1), 'expert', split_...  17.9 us
  transfers between devices with their start and end apart: 17, of which 15 were waited for; matrix products, arithmetic and copies ran while one was open for 28% of the time, Pallas kernels for 0%

profile of v1, /device:TPU:2, one launch (start us, length us, event | category | flops | bytes accessed | tf_op | source)
XLA Modules:
  0.0 746.1 jit_solution(8509542572352011516)
XLA Ops:
  26.6 16.0 %all-to-all-start.1 = ((bf16[128,8,1024]{2,1,0:T(8,128)(2,1)}), bf16[128,8,1024]{2,1,0:T(8,128)(2,1)}, u32[]{:S(2)}, u32[]{:S(2)}) async-start(bf16[128,8,1024]{2,1,0:T(8,128)(2,1)} %bitcast_select_fusion), calls=%async_computation.1 | async-start | bytes 4194304 | tf_op jit(solution)/shard_map/all_to_all | solution.py:190
  48.6 46.3 %all-to-all-done.1 = bf16[128,8,1024]{2,1,0:T(8,128)(2,1)} async-done(((bf16[128,8,1024]{2,1,0:T(8,128)(2,1)}), bf16[128,8,1024]{2,1,0:T(8,128)(2,1)}, u32[]{:S(2)}, u32[]{:S(2)}) %all-to-all-start.1) | async-done | bytes 2097184 | tf_op jit(solution)/shard_map/all_to_all | solution.py:190
  94.9 7.2 all-to-all-start
  107.7 46.3 %all-to-all-done = bf16[128,8,1024]{2,1,0:T(8,128)(2,1)S(1)} async-done(((bf16[128,8,1024]{2,1,0:T(8,128)(2,1)}), bf16[128,8,1024]{2,1,0:T(8,128)(2,1)S(1)}, u32[]{:S(2)}, u32[]{:S(2)}) %all-to-all-start) | async-done | bytes 2097184 | tf_op jit(solution)/shard_map/all_to_all | solution.py:183
  168.9 16.3 %reduce-scatter.3.cloned.1.call-done = bf16[512,768]{1,0:T(8,128)(2,1)} async-done(((bf16[1024,768]{1,0:T(8,128)(2,1)}), bf16[512,768]{1,0:T(8,128)(2,1)}) %reduce-scatter.3.cloned.1.call-update) | async-done | bytes 786448 | tf_op jit(solution)/shard_map/reduce_scatter | solution.py:217
  203.6 14.8 %all-to-all-start.5 = ((bf16[128,2,768]{2,1,0:T(2,128)(2,1)}), bf16[128,2,768]{2,1,0:T(2,128)(2,1)}, u32[]{:S(2)}, u32[]{:S(2)}) async-start(bf16[128,2,768]{2,1,0:T(2,128)(2,1)} %reshape.474), calls=%async_computation.7 | async-start | bytes 786432 | tf_op jit(solution)/shard_map/all_to_all | solution.py:132
  288.1 13.7 %all-to-all-start.2 = ((bf16[128,8,1024]{2,1,0:T(8,128)(2,1)}), bf16[128,8,1024]{2,1,0:T(8,128)(2,1)S(1)}, u32[]{:S(2)}, u32[]{:S(2)}) async-start(bf16[128,8,1024]{2,1,0:T(8,128)(2,1)} %convert_bitcast_fusion), calls=%async_computation.2 | async-start | bytes 4194304 | tf_op jit(solution)/shard_map/all_to_all | solution.py:204
  315.4 39.1 %all-to-all-done.2 = bf16[128,8,1024]{2,1,0:T(8,128)(2,1)S(1)} async-done(((bf16[128,8,1024]{2,1,0:T(8,128)(2,1)}), bf16[128,8,1024]{2,1,0:T(8,128)(2,1)S(1)}, u32[]{:S(2)}, u32[]{:S(2)}) %all-to-all-start.2) | async-done | bytes 2097184 | tf_op jit(solution)/shard_map/all_to_all | solution.py:204
  354.5 7.6 %all-to-all-start.13 = ((f32[1,128,1536]{2,0,1:T(1,128)}), f32[1,128,1536]{2,0,1:T(1,128)}, u32[]{:S(2)}, u32[]{:S(2)}) async-start(f32[1,128,1536]{2,0,1:T(1,128)} %reshape.460), calls=%async_computation.15 | async-start | bytes 1572864 | tf_op jit(solution)/shard_map/all_to_all | solution.py:103
  368.4 17.9 %all-to-all-done.13 = f32[1,128,1536]{2,0,1:T(1,128)} async-done(((f32[1,128,1536]{2,0,1:T(1,128)}), f32[1,128,1536]{2,0,1:T(1,128)}, u32[]{:S(2)}, u32[]{:S(2)}) %all-to-all-start.13) | async-done | bytes 786464 | tf_op jit(solution)/shard_map/all_to_all | solution.py:103
  386.3 8.0 %all-to-all-start.11 = ((f32[1,128,1536]{2,0,1:T(1,128)}), f32[1,128,1536]{2,0,1:T(1,128)}, u32[]{:S(2)}, u32[]{:S(2)}) async-start(f32[1,128,1536]{2,0,1:T(1,128)} %reshape.458), calls=%async_computation.13 | async-start | bytes 1572864 | tf_op jit(solution)/shard_map/all_to_all | solution.py:96
  406.0 11.4 %all-to-all-done.11 = f32[1,128,1536]{2,0,1:T(1,128)} async-done(((f32[1,128,1536]{2,0,1:T(1,128)}), f32[1,128,1536]{2,0,1:T(1,128)}, u32[]{:S(2)}, u32[]{:S(2)}) %all-to-all-start.11) | async-done | bytes 786464 | tf_op jit(solution)/shard_map/all_to_all | solution.py:96
  432.3 14.6 %all-to-all-done.3 = bf16[128,2,1536]{2,1,0:T(2,128)(2,1)S(1)} async-done(((bf16[128,2,1536]{2,1,0:T(2,128)(2,1)}), bf16[128,2,1536]{2,1,0:T(2,128)(2,1)S(1)}, u32[]{:S(2)}, u32[]{:S(2)}) %all-to-all-start.3) | async-done | bytes 786464 | tf_op jit(solution)/shard_map/all_to_all | solution.py:129
  468.5 7.7 %all-to-all-start.14 = ((f32[128,1,1536]{2,1,0:T(1,128)}), f32[128,1,1536]{2,1,0:T(1,128)S(1)}, u32[]{:S(2)}, u32[]{:S(2)}) async-start(f32[128,1,1536]{2,1,0:T(1,128)} %copy.74), calls=%async_computation.16 | async-start | bytes 1572864 | tf_op jit(solution)/shard_map/all_to_all | solution.py:116
  482.4 15.8 %all-to-all-done.14 = f32[128,1,1536]{2,1,0:T(1,128)S(1)} async-done(((f32[128,1,1536]{2,1,0:T(1,128)}), f32[128,1,1536]{2,1,0:T(1,128)S(1)}, u32[]{:S(2)}, u32[]{:S(2)}) %all-to-all-start.14) | async-done | bytes 786464 | tf_op jit(solution)/shard_map/all_to_all | solution.py:116
  509.4 17.1 %all-to-all-done.12 = f32[128,1,1536]{2,1,0:T(1,128)S(1)} async-done(((f32[128,1,1536]{2,1,0:T(1,128)}), f32[128,1,1536]{2,1,0:T(1,128)S(1)}, u32[]{:S(2)}, u32[]{:S(2)}) %all-to-all-start.12) | async-done | bytes 786464 | tf_op jit(solution)/shard_map/all_to_all | solution.py:115
  536.8 34.4 %all-to-all-done.7 = f32[128,1,1,3072]{3,2,1,0:T(1,128)S(1)} async-done(((f32[128,1,1,3072]{3,2,1,0:T(1,128)}), f32[128,1,1,3072]{3,2,1,0:T(1,128)S(1)}, u32[]{:S(2)}, u32[]{:S(2)}) %all-to-all-start.7) | async-done | bytes 1572896 | tf_op jit(solution)/shard_map/all_to_all | solution.py:77
  571.2 7.9 %all-to-all-start.9 = ((f32[1,128,3072]{2,0,1:T(1,128)}), f32[1,128,3072]{2,0,1:T(1,128)}, u32[]{:S(2)}, u32[]{:S(2)}) async-start(f32[1,128,3072]{2,0,1:T(1,128)} %reshape.456), calls=%async_computation.11 | async-start | bytes 3145728 | tf_op jit(solution)/shard_map/all_to_all | solution.py:89
  586.6 29.2 %all-to-all-done.9 = f32[1,128,3072]{2,0,1:T(1,128)} async-done(((f32[1,128,3072]{2,0,1:T(1,128)}), f32[1,128,3072]{2,0,1:T(1,128)}, u32[]{:S(2)}, u32[]{:S(2)}) %all-to-all-start.9) | async-done | bytes 1572896 | tf_op jit(solution)/shard_map/all_to_all | solution.py:89
  615.7 7.4 all-to-all-start.4
  633.2 11.0 %all-to-all-done.4 = bf16[128,2,1536]{2,1,0:T(2,128)(2,1)} async-done(((bf16[128,2,1536]{2,1,0:T(2,128)(2,1)}), bf16[128,2,1536]{2,1,0:T(2,128)(2,1)}, u32[]{:S(2)}, u32[]{:S(2)}) %all-to-all-start.4) | async-done | bytes 786464 | tf_op jit(solution)/shard_map/all_to_all | solution.py:142
  644.2 7.7 %all-to-all-start.10 = ((f32[128,1,3072]{2,1,0:T(1,128)}), f32[128,1,3072]{2,1,0:T(1,128)}, u32[]{:S(2)}, u32[]{:S(2)}) async-start(f32[128,1,3072]{2,1,0:T(1,128)} %copy.70), calls=%async_computation.12 | async-start | bytes 3145728 | tf_op jit(solution)/shard_map/all_to_all | solution.py:114
  654.6 33.3 %all-to-all-done.10 = f32[128,1,3072]{2,1,0:T(1,128)} async-done(((f32[128,1,3072]{2,1,0:T(1,128)}), f32[128,1,3072]{2,1,0:T(1,128)}, u32[]{:S(2)}, u32[]{:S(2)}) %all-to-all-start.10) | async-done | bytes 1572896 | tf_op jit(solution)/shard_map/all_to_all | solution.py:114
  687.9 7.6 %all-to-all-start.8 = ((f32[128,1,3072]{2,1,0:T(1,128)}), f32[128,1,3072]{2,1,0:T(1,128)}, u32[]{:S(2)}, u32[]{:S(2)}) async-start(f32[128,1,3072]{2,1,0:T(1,128)} %copy.68), calls=%async_computation.10 | async-start | bytes 3145728 | tf_op jit(solution)/shard_map/all_to_all | solution.py:113
  (287 shorter events, 290.6 us)
Async XLA Ops:
  26.6 68.3 %all-to-all-start.1 = ((bf16[128,8,1024]{2,1,0:T(8,128)(2,1)}), bf16[128,8,1024]{2,1,0:T(8,128)(2,1)}, u32[]{:S(2)}, u32[]{:S(2)}) async-start(bf16[128,8,1024]{2,1,0:T(8,128)(2,1)} %bitcast_select_fusion), calls=%async_computation.1 | async-start | bytes 4194304 | tf_op jit(solution)/shard_map/all_to_all | solution.py:190
  94.9 59.1 %all-to-all-start = ((bf16[128,8,1024]{2,1,0:T(8,128)(2,1)}), bf16[128,8,1024]{2,1,0:T(8,128)(2,1)S(1)}, u32[]{:S(2)}, u32[]{:S(2)}) async-start(bf16[128,8,1024]{2,1,0:T(8,128)(2,1)} %fusion), calls=%async_computation | async-start | bytes 4194304 | tf_op jit(solution)/shard_map/all_to_all | solution.py:183
  102.2 65.1 %reduce-scatter.5.cloned.1.call-start = ((), (), s32[]{:S(2)}) async-start(), calls=%async_computation.18 | async-start | bytes 1179648 | tf_op jit(solution)/shard_map/reduce_scatter | solution.py:220
  107.7 50.4 %copy-start.21 = (bf16[1,384,1024]{2,1,0:T(8,128)(2,1)S(1)}, bf16[1,384,1024]{2,1,0:T(8,128)(2,1)}, u32[]{:S(2)}) copy-start(bf16[1,384,1024]{2,1,0:T(8,128)(2,1)} %param.20) | copy-start | bytes 2359300
  157.8 27.4 %reduce-scatter.3.cloned.1.call-start = ((), (), s32[]{:S(2)}) async-start(), calls=%async_computation.17 | async-start | bytes 2359296 | tf_op jit(solution)/shard_map/reduce_scatter | solution.py:217
  203.6 84.5 %all-to-all-start.5 = ((bf16[128,2,768]{2,1,0:T(2,128)(2,1)}), bf16[128,2,768]{2,1,0:T(2,128)(2,1)}, u32[]{:S(2)}, u32[]{:S(2)}) async-start(bf16[128,2,768]{2,1,0:T(2,128)(2,1)} %reshape.474), calls=%async_computation.7 | async-start | bytes 786432 | tf_op jit(solution)/shard_map/all_to_all | solution.py:132
  223.6 64.5 %copy-start.5 = (f32[1,128,3072]{2,1,0:T(8,128)}, f32[1,128,3072]{2,1,0:T(8,128)S(1)}, u32[]{:S(2)}) copy-start(f32[1,128,3072]{2,1,0:T(8,128)S(1)} %reshape.320) | copy-start | bytes 4718596
  288.1 66.4 %all-to-all-start.2 = ((bf16[128,8,1024]{2,1,0:T(8,128)(2,1)}), bf16[128,8,1024]{2,1,0:T(8,128)(2,1)S(1)}, u32[]{:S(2)}, u32[]{:S(2)}) async-start(bf16[128,8,1024]{2,1,0:T(8,128)(2,1)} %convert_bitcast_fusion), calls=%async_computation.2 | async-start | bytes 4194304 | tf_op jit(solution)/shard_map/all_to_all | solution.py:204
  303.4 60.2 %copy-start.7 = (f32[384,512]{1,0:T(8,128)S(1)}, f32[384,512]{1,0:T(8,128)}, u32[]{:S(2)}) copy-start(f32[384,512]{1,0:T(8,128)} %get-tuple-element.11) | copy-start | bytes 2359300
  354.5 31.9 %all-to-all-start.13 = ((f32[1,128,1536]{2,0,1:T(1,128)}), f32[1,128,1536]{2,0,1:T(1,128)}, u32[]{:S(2)}, u32[]{:S(2)}) async-start(f32[1,128,1536]{2,0,1:T(1,128)} %reshape.460), calls=%async_computation.15 | async-start | bytes 1572864 | tf_op jit(solution)/shard_map/all_to_all | solution.py:103
  365.4 30.5 %copy-start.8 = (bf16[512,768]{1,0:T(8,128)(2,1)S(1)}, bf16[512,768]{1,0:T(8,128)(2,1)}, u32[]{:S(2)}) copy-start(bf16[512,768]{1,0:T(8,128)(2,1)} %get-tuple-element.14) | copy-start | bytes 2359300
  386.3 31.1 %all-to-all-start.11 = ((f32[1,128,1536]{2,0,1:T(1,128)}), f32[1,128,1536]{2,0,1:T(1,128)}, u32[]{:S(2)}, u32[]{:S(2)}) async-start(f32[1,128,1536]{2,0,1:T(1,128)} %reshape.458), calls=%async_computation.13 | async-start | bytes 1572864 | tf_op jit(solution)/shard_map/all_to_all | solution.py:96
  417.4 29.5 %all-to-all-start.3 = ((bf16[128,2,1536]{2,1,0:T(2,128)(2,1)}), bf16[128,2,1536]{2,1,0:T(2,128)(2,1)S(1)}, u32[]{:S(2)}, u32[]{:S(2)}) async-start(bf16[128,2,1536]{2,1,0:T(2,128)(2,1)} %reshape.470), calls=%async_computation.5 | async-start | bytes 1572864 | tf_op jit(solution)/shard_map/all_to_all | solution.py:129
  446.9 21.6 %all-to-all-start.6 = ((bf16[128,2,768]{2,1,0:T(2,128)(2,1)}), bf16[128,2,768]{2,1,0:T(2,128)(2,1)S(1)}, u32[]{:S(2)}, u32[]{:S(2)}) async-start(bf16[128,2,768]{2,1,0:T(2,128)(2,1)} %reshape.476), calls=%async_computation.8 | async-start | bytes 786432 | tf_op jit(solution)/shard_map/all_to_all | solution.py:143
  468.5 29.7 %all-to-all-start.14 = ((f32[128,1,1536]{2,1,0:T(1,128)}), f32[128,1,1536]{2,1,0:T(1,128)S(1)}, u32[]{:S(2)}, u32[]{:S(2)}) async-start(f32[128,1,1536]{2,1,0:T(1,128)} %copy.74), calls=%async_computation.16 | async-start | bytes 1572864 | tf_op jit(solution)/shard_map/all_to_all | solution.py:116
  498.2 28.3 %all-to-all-start.12 = ((f32[128,1,1536]{2,1,0:T(1,128)}), f32[128,1,1536]{2,1,0:T(1,128)S(1)}, u32[]{:S(2)}, u32[]{:S(2)}) async-start(f32[128,1,1536]{2,1,0:T(1,128)} %copy.72), calls=%async_computation.14 | async-start | bytes 1572864 | tf_op jit(solution)/shard_map/all_to_all | solution.py:115
  509.4 24.7 %copy-start.6 = (f32[512,768]{1,0:T(8,128)S(1)}, f32[512,768]{1,0:T(8,128)}, u32[]{:S(2)}) copy-start(f32[512,768]{1,0:T(8,128)} %get-tuple-element.15) | copy-start | bytes 4718596
  527.4 43.9 %all-to-all-start.7 = ((f32[128,1,1,3072]{3,2,1,0:T(1,128)}), f32[128,1,1,3072]{3,2,1,0:T(1,128)S(1)}, u32[]{:S(2)}, u32[]{:S(2)}) async-start(f32[128,1,1,3072]{3,2,1,0:T(1,128)} %constant_dynamic-update-slice_fusion), calls=%async_computation.9 | async-start | bytes 3145728 | tf_op jit(solution)/shard_map/all_to_all | solution.py:77
  536.8 42.3 %copy-start.15 = (bf16[128,2,1536]{2,1,0:T(2,128)(2,1)S(1)}, bf16[128,2,1536]{2,1,0:T(2,128)(2,1)}, u32[]{:S(2)}) copy-start(bf16[128,2,1536]{2,1,0:T(2,128)(2,1)} %copy-done.14) | copy-start | bytes 2359300
  571.2 44.5 %all-to-all-start.9 = ((f32[1,128,3072]{2,0,1:T(1,128)}), f32[1,128,3072]{2,0,1:T(1,128)}, u32[]{:S(2)}, u32[]{:S(2)}) async-start(f32[1,128,3072]{2,0,1:T(1,128)} %reshape.456), calls=%async_computation.11 | async-start | bytes 3145728 | tf_op jit(solution)/shard_map/all_to_all | solution.py:89
  615.7 28.4 %all-to-all-start.4 = ((bf16[128,2,1536]{2,1,0:T(2,128)(2,1)}), bf16[128,2,1536]{2,1,0:T(2,128)(2,1)}, u32[]{:S(2)}, u32[]{:S(2)}) async-start(bf16[128,2,1536]{2,1,0:T(2,128)(2,1)} %reshape.472), calls=%async_computation.6 | async-start | bytes 1572864 | tf_op jit(solution)/shard_map/all_to_all | solution.py:142
  644.2 43.8 %all-to-all-start.10 = ((f32[128,1,3072]{2,1,0:T(1,128)}), f32[128,1,3072]{2,1,0:T(1,128)}, u32[]{:S(2)}, u32[]{:S(2)}) async-start(f32[128,1,3072]{2,1,0:T(1,128)} %copy.70), calls=%async_computation.12 | async-start | bytes 3145728 | tf_op jit(solution)/shard_map/all_to_all | solution.py:114
  654.6 41.0 %copy-start.4 = (bf16[128,8,1024]{2,1,0:T(8,128)(2,1)S(1)}, bf16[128,8,1024]{2,1,0:T(8,128)(2,1)}, u32[]{:S(2)}) copy-start(bf16[128,8,1024]{2,1,0:T(8,128)(2,1)} %copy-done.3) | copy-start | bytes 6291460
  687.9 44.2 %all-to-all-start.8 = ((f32[128,1,3072]{2,1,0:T(1,128)}), f32[128,1,3072]{2,1,0:T(1,128)}, u32[]{:S(2)}, u32[]{:S(2)}) async-start(f32[128,1,3072]{2,1,0:T(1,128)} %copy.68), calls=%async_computation.10 | async-start | bytes 3145728 | tf_op jit(solution)/shard_map/all_to_all | solution.py:113
  (17 other events, 159.4 us)
Sparse Core Ops, SparseCore 0:
  158.0 8.2 reduce-scatter.4
  169.5 15.7 reduce-scatter.2
